TPU v7x, 32 devices: a whole 2x2x4 slice. The times are simulated.
32 devices in a mesh: frow: 4 (over x, core), fcol: 8 (over z, y).
Axes of the slice: x: 2, y: 2, z: 4, core: 2. Of those that a mesh axis runs over, the one named last changes fastest.
Arguments:
- facet_image: bfloat16 [2048, 4096], P('frow', 'fcol'), may hold values from -6 to 6
- row_offsets: int32 [2], replicated, may hold values from 0 to 65280
- col_offsets: int32 [2], replicated, may hold values from 0 to 65280
- vis_subgrid: int32 [16384], P(('frow', 'fcol')), may hold values from 0 to 3
- vis_u: int32 [16384], P(('frow', 'fcol')), may hold values from 0 to 255
- vis_v: int32 [16384], P(('frow', 'fcol')), may hold values from 0 to 255
- observed: float32 [2, 16384], P(None, ('frow', 'fcol')), may hold values from -6 to 6
Outputs:
- facet_residual: float32 [2048, 4096], P('frow', 'fcol')
- residual_vis: float32 [2, 16384], P(None, ('frow', 'fcol'))
Inputs may be any that keep to these rules, and one draw needn't show every extreme that they name: `vis_subgrid`: subgrid numbers count row by row over the 2 x 2 subgrids.
All inputs are finite; a program needn't handle non-finite values.
Results may differ from a plain program's by a relative error of at most 0.023.
Values may be sent and summed in bfloat16 or wider, within the bound.
A program may use at most 64 MiB of HBM per device.

v0:
```python
import math
import jax
import jax.numpy as jnp
from jax import lax
from jax.sharding import PartitionSpec as P

SKY = 65536
SG = 256
NR = 2
NC = 2


def wrapped(frequency, position):
    high_part = frequency // 256
    low_part = frequency % 256
    return (high_part * (position * 256 % SKY) + low_part * position) % SKY


def sky_tables(start, positions):
    frequency = start + jnp.arange(SG, dtype=jnp.int32)[:, None]
    angles = wrapped(frequency, positions[None, :]).astype(jnp.float32) * (2.0 * math.pi / SKY)
    return (jnp.cos(angles).astype(jnp.bfloat16), jnp.sin(angles).astype(jnp.bfloat16))


def grid_tables():
    counter = jnp.arange(SG, dtype=jnp.int32)
    angles = (counter[:, None] * counter[None, :] % SG).astype(jnp.float32) * (2.0 * math.pi / SG)
    return (jnp.cos(angles).astype(jnp.bfloat16), jnp.sin(angles).astype(jnp.bfloat16))


def contract_first(left, right):
    return lax.dot_general(
        left, right, (((0,), (0,)), ((), ())), preferred_element_type=jnp.float32
    )


def contract_last(left, right):
    return lax.dot_general(
        left, right, (((1,), (1,)), ((), ())), preferred_element_type=jnp.float32
    )


def shards(facet_image, row_offsets, col_offsets, vis_subgrid, vis_u, vis_v, observed):
    f32 = jnp.float32
    bf16 = jnp.bfloat16
    rows_count = lax.axis_size("frow")
    cols_count = lax.axis_size("fcol")
    facet_side = facet_image.shape[0]
    subgrids = NR * NC
    scale_in = 1.0 / (facet_side * math.sqrt(rows_count * cols_count))
    scale_out = 1.0 / (SG * math.sqrt(subgrids))
    row_pos = lax.axis_index("frow") * (SKY // rows_count) + jnp.arange(
        facet_side, dtype=jnp.int32
    ) * (SKY // (rows_count * facet_side))
    col_pos = lax.axis_index("fcol") * (SKY // cols_count) + jnp.arange(
        facet_side, dtype=jnp.int32
    ) * (SKY // (cols_count * facet_side))
    row_tabs = [
        jnp.concatenate(sky_tables(row_offsets[row_pick], row_pos), 0) for row_pick in range(NR)
    ]
    col_tabs = [
        jnp.concatenate(sky_tables(col_offsets[col_pick], col_pos), 0) for col_pick in range(NC)
    ]
    col_halves = [
        contract_last(facet_image, col_tabs[col_pick]).astype(bf16) for col_pick in range(NC)
    ]
    blocks_out = []
    for row_pick in range(NR):
        for col_pick in range(NC):
            product = jnp.dot(row_tabs[row_pick], col_halves[col_pick], preferred_element_type=f32)
            part_real = product[:SG, :SG] - product[SG:, SG:]
            part_imag = -(product[:SG, SG:] + product[SG:, :SG])
            blocks_out.append(jnp.concatenate([part_real, part_imag], 1) * scale_in)
    stacked = jnp.concatenate(blocks_out, 0)
    summed = lax.psum(stacked, ("frow", "fcol"))
    grid_bf = summed.astype(bf16)
    kcos, ksin = grid_tables()
    forward_block = jnp.concatenate(
        [jnp.concatenate([kcos, ksin], 1), jnp.concatenate([-ksin, kcos], 1)], 0
    )
    w_both = (
        jnp.dot(grid_bf, forward_block, preferred_element_type=f32)
        .astype(bf16)
        .reshape(subgrids, SG, 2 * SG)
    )
    with_cos = jnp.einsum("au,sav->suv", kcos, w_both, preferred_element_type=f32)
    with_sin = jnp.einsum("au,sav->suv", ksin, w_both, preferred_element_type=f32)
    hat_real = (with_cos[:, :, :SG] - with_sin[:, :, SG:]) / SG
    hat_imag = (with_sin[:, :, :SG] + with_cos[:, :, SG:]) / SG
    cell_ids = (vis_subgrid * SG + vis_u) * SG + vis_v
    model_vis = jnp.stack(
        [jnp.take(hat_real.reshape(-1), cell_ids), jnp.take(hat_imag.reshape(-1), cell_ids)]
    )
    residual = observed - model_vis
    cells_all = subgrids * SG * SG
    inverse_block = jnp.concatenate(
        [jnp.concatenate([kcos, -ksin], 1), jnp.concatenate([ksin, kcos], 1)], 0
    )
    local_real = jax.ops.segment_sum(residual[0], cell_ids, num_segments=cells_all)
    local_imag = jax.ops.segment_sum(residual[1], cell_ids, num_segments=cells_all)
    ghat_real, ghat_imag = lax.psum((local_real, local_imag), ("frow", "fcol"))
    ghat_both = jnp.concatenate(
        [
            ghat_real.reshape(subgrids * SG, SG).astype(bf16),
            ghat_imag.reshape(subgrids * SG, SG).astype(bf16),
        ],
        1,
    )
    v_flat = jnp.dot(ghat_both, inverse_block, preferred_element_type=f32).astype(bf16)
    v_both = v_flat.reshape(subgrids, SG, 2 * SG)
    back_cos = jnp.einsum("au,suv->sav", kcos, v_both, preferred_element_type=f32)
    back_sin = jnp.einsum("au,suv->sav", ksin, v_both, preferred_element_type=f32)
    back_real = ((back_cos[:, :, :SG] + back_sin[:, :, SG:]) / SG).astype(bf16)
    back_imag = ((back_cos[:, :, SG:] - back_sin[:, :, :SG]) / SG).astype(bf16)
    image = jnp.zeros((facet_side, facet_side), f32)
    for col_pick in range(NC):
        u_both = jnp.zeros((facet_side, 2 * SG), f32)
        for row_pick in range(NR):
            sub_index = row_pick * NC + col_pick
            g_real = back_real[sub_index]
            g_imag = back_imag[sub_index]
            right_side = jnp.concatenate(
                [jnp.concatenate([g_real, g_imag], 1), jnp.concatenate([-g_imag, g_real], 1)], 0
            )
            u_both = u_both + contract_first(row_tabs[row_pick], right_side)
        col_cos = col_tabs[col_pick][:SG]
        col_sin = col_tabs[col_pick][SG:]
        image = image + jnp.dot(
            u_both.astype(bf16), jnp.concatenate([col_cos, -col_sin], 0), preferred_element_type=f32
        )
    return (image * scale_out, residual)


def solution(mesh):
    in_specs = (
        P("frow", "fcol"),
        P(),
        P(),
        P(("frow", "fcol")),
        P(("frow", "fcol")),
        P(("frow", "fcol")),
        P(None, ("frow", "fcol")),
    )
    out_specs = (P("frow", "fcol"), P(None, ("frow", "fcol")))
    return jax.shard_map(shards, mesh=mesh, in_specs=in_specs, out_specs=out_specs, check_vma=False)
```

profile of v0, /device:TPU:0, one launch (start us, length us, event | category | flops | bytes accessed | tf_op | source)
XLA Modules:
  0.0 194.2 jit_solution(18069458550596602750)
XLA Ops:
  0.7 1.3 fusion.145
  2.0 0.7 and_select_fusion.4
  2.7 0.7 and_select_fusion.2
  3.3 4.6 %sine_convert_fusion.2 = (bf16[256,512]{1,0:T(8,128)(2,1)S(1)}, bf16[256,512]{1,0:T(8,128)(2,1)S(1)}, bf16[256,512]{1,0:T(8,128)(2,1)S(1)}, bf16[256,512]{1,0:T(8,128)(2,1)S(1)}) fusion(s32[512]{0:T(512)S(1)} %get-tuple-element.54, s32[256]{0:T(256)S(1)} %get-tuple-element.55, s32[512]{0:T(512)S(1)} %get-tuple-element.53, s32[256]{0:T(256)S(1)} %get-tuple-element.56, ...), kind=kLoop, calls=%fused_computation.116 | loop fusion | flops 4718592 | bytes 1056768 | tf_op jit(solution)/shard_map/convert_element_type | solution.py:22
  8.0 0.7 copy-done.5
  9.8 0.7 and_select_fusion.6
  10.4 0.7 and_select_fusion
  11.1 4.6 %cosine_convert_fusion.3 = (bf16[256,512]{1,0:T(8,128)(2,1)S(1)}, bf16[256,512]{1,0:T(8,128)(2,1)S(1)}, bf16[256,512]{1,0:T(8,128)(2,1)S(1)}, bf16[256,512]{1,0:T(8,128)(2,1)S(1)}) fusion(s32[512]{0:T(512)S(1)} %get-tuple-element.60, s32[256]{0:T(256)S(1)} %get-tuple-element.61, s32[512]{0:T(512)S(1)} %get-tuple-element.59, s32[256]{0:T(256)S(1)} %get-tuple-element.62, ...), kind=kLoop, calls=%fused_computation.123 | loop fusion | flops 4718592 | bytes 1056768 | tf_op jit(solution)/shard_map/convert_element_type | solution.py:22
  19.0 64.4 %all-reduce.3 = bf16[1024,512]{0,1:T(8,128)(2,1)} all-reduce(f32[1024,512]{0,1:T(8,128)S(1)} %pad_maximum_fusion), channel_id=1, replica_groups=mesh['frow'=4,'fcol'=8] {'frow','fcol'}, use_global_device_ids=true, to_apply=%region_0.1 | all-reduce | flops 524288 | bytes 3145728 | tf_op jit(solution)/shard_map/psum | solution.py:75
  83.4 1.1 sine_convert_fusion.4
  84.5 1.0 fusion.100
  85.5 2.0 %convolution_convert_fusion.1 = bf16[1024,512]{1,0:T(8,128)(2,1)S(1)} fusion(bf16[1024,512]{0,1:T(8,128)(2,1)} %all-reduce.3, bf16[256,256]{1,0:T(8,128)(2,1)S(1)} %get-tuple-element.66, bf16[256,256]{1,0:T(8,128)(2,1)S(1)} %fusion.100, bf16[256,256]{1,0:T(8,128)(2,1)S(1)} %get-tuple-element.65), kind=kOutput, calls=%fused_computation.10 | convolution fusion | flops 539492352 | bytes 2490368 | tf_op jit(solution)/shard_map/dot_general | solution.py:82
  87.5 1.4 convolution_bitcast_fusion.2
  88.9 1.4 convolution_bitcast_fusion.3
  90.3 1.3 fusion.9
  93.3 4.3 %gather_fusion.1 = f32[512]{0:T(512)} fusion(f32[262144]{0:T(1024)S(1)} %bitcast.67, s32[1024]{0:T(1024)S(1)} %pad_clamp_fusion), kind=kCustom, calls=%fused_computation.1.clone | custom fusion | bytes 6144 | tf_op jit(solution)/shard_map/jit(_take)/gather | solution.py:92
  97.5 1.6 copy.15
  99.7 3.1 %gather_fusion = f32[512]{0:T(512)S(1)} fusion(f32[262144]{0:T(1024)S(1)} %bitcast.68, s32[1024]{0:T(1024)S(1)} %pad_clamp_fusion), kind=kCustom, calls=%fused_computation.clone | custom fusion | bytes 6144 | tf_op jit(solution)/shard_map/jit(_take)/gather | solution.py:92
  103.5 3.5 %scatter_custom_fusion = f32[262144]{0:T(1024)S(1)} fusion(s32[512]{0:T(512)S(1)} %copy-done.18, f32[512]{0:T(512)S(1)} %bitcast.78, f32[]{:T(128)} %constant.156.clone.1), kind=kCustom, calls=%fused_computation.120 | custom fusion | flops 512 | bytes 1048580 | tf_op jit(solution)/shard_map/scatter-add | solution.py:99
  107.0 3.7 %scatter_custom_fusion.1 = f32[262144]{0:T(1024)S(1)} fusion(s32[512]{0:T(512)} %get-tuple-element.6, f32[512]{0:T(512)} %bitcast.77, f32[]{:T(128)} %constant.156.clone.1), kind=kCustom, calls=%fused_computation.118 | custom fusion | flops 512 | bytes 1049088 | tf_op jit(solution)/shard_map/scatter-add | solution.py:100
  110.7 62.5 %all-reduce.4 = (bf16[262144]{0:T(1024)(128)(2,1)}, bf16[262144]{0:T(1024)(128)(2,1)}) all-reduce(f32[262144]{0:T(1024)S(1)} %scatter_custom_fusion.1, f32[262144]{0:T(1024)S(1)} %scatter_custom_fusion), channel_id=1, replica_groups=mesh['frow'=4,'fcol'=8] {'frow','fcol'}, use_global_device_ids=true, to_apply=%region_4.6 | all-reduce | flops 524288 | bytes 3145728 | tf_op jit(solution)/shard_map/psum | solution.py:101
  173.2 1.3 convert_element_type.148
  174.4 1.2 convert_element_type.150
  175.7 0.7 convolution_convert_fusion
  176.4 1.4 convolution_bitcast_fusion
  177.8 1.4 convolution_bitcast_fusion.1
  179.7 0.8 copy-done.2
  180.6 1.5 fusion.59
  182.0 1.5 fusion.36
  183.5 4.4 %fusion.138 = (bf16[256,512]{1,0:T(8,128)(2,1)S(1)}, bf16[256,512]{1,0:T(8,128)(2,1)S(1)}) fusion(s32[512]{0:T(512)S(1)} %get-tuple-element.54, s32[256]{0:T(256)S(1)} %copy-done.15, s32[512]{0:T(512)S(1)} %get-tuple-element.53, s32[256]{0:T(256)S(1)} %copy-done.17, s32[256]{0:T(256)S(1)} %get-tuple-element.55, s32[256]{0:T(256)S(1)} %copy-done.13), kind=kLoop, calls=%fused_computation.238 | loop fusion | flops 5242880 | bytes 532480 | tf_op jit(solution)/shard_map/neg | solution.py:129
  187.9 3.0 %fusion.3 = f32[512,512]{1,0:T(8,128)} fusion(f32[512,512]{1,0:T(8,128)} %fusion.36, bf16[256,512]{1,0:T(8,128)(2,1)S(1)} %copy-done.6, bf16[256,256]{0,1:T(8,128)(2,1)S(1)} %get-tuple-element.29, bf16[256,256]{0,1:T(8,128)(2,1)S(1)} %get-tuple-element.25, bf16[256,256]{0,1:T(8,128)(2,1)S(1)} %get-tuple-element.21, ...), kind=kOutput, calls=%fused_computation.19 | convolution fusion | flops 541589504 | bytes 3538944 | tf_op jit(solution)/shard_map/dot_general | solution.py:128
  190.9 3.3 %fusion = f32[512,512]{1,0:T(8,128)} fusion(f32[512,512]{1,0:T(8,128)} %fusion.3, f32[512,512]{1,0:T(8,128)} %fusion.59, bf16[256,512]{1,0:T(8,128)(2,1)S(1)} %copy-done.4, bf16[256,256]{0,1:T(8,128)(2,1)S(1)} %get-tuple-element.27, bf16[256,256]{0,1:T(8,128)(2,1)S(1)} %get-tuple-element.23, bf16[256,256]{0,1:T(8,128)(2,1)S(1)} %get-tuple-element.19, ...), kind=kOutput, calls=%fused_computation.12 | convolution fusion | flops 542113792 | bytes 4587520 | tf_op jit(solution)/shard_map/dot_general | solution.py:128
  (78 shorter events, 7.5 us)
Async XLA Ops:
  0.6 8.1 %copy-start = (bf16[512,512]{1,0:T(8,128)(2,1)S(1)}, bf16[512,512]{1,0:T(8,128)(2,1)}, u32[]{:S(2)}) copy-start(bf16[512,512]{1,0:T(8,128)(2,1)} %param.9) | copy-start | bytes 1572868
  0.6 8.5 %copy-start.24 = (s32[2]{0:T(128)S(1)}, s32[2]{0:T(128)}, u32[]{:S(2)}) copy-start(s32[2]{0:T(128)} %param.10) | copy-start | bytes 28
  2.7 13.6 %copy-start.12 = (s32[256]{0:T(256)}, s32[256]{0:T(256)S(1)}, u32[]{:S(2)}) copy-start(s32[256]{0:T(256)S(1)} %get-tuple-element.56) | copy-start | bytes 3076
  3.3 12.9 %copy-start.14 = (s32[256]{0:T(256)}, s32[256]{0:T(256)S(1)}, u32[]{:S(2)}) copy-start(s32[256]{0:T(256)S(1)} %get-tuple-element.57) | copy-start | bytes 3076
  3.3 12.9 %copy-start.16 = (s32[256]{0:T(256)}, s32[256]{0:T(256)S(1)}, u32[]{:S(2)}) copy-start(s32[256]{0:T(256)S(1)} %get-tuple-element.58) | copy-start | bytes 3076
  8.0 0.7 copy-start.5
  8.0 8.4 %copy-start.3 = (bf16[256,512]{1,0:T(8,128)(2,1)}, bf16[256,512]{1,0:T(8,128)(2,1)S(1)}, u32[]{:S(2)}) copy-start(bf16[256,512]{1,0:T(8,128)(2,1)S(1)} %get-tuple-element.45) | copy-start | bytes 786436
  15.7 1.1 copy-start.1
  84.5 3.0 %copy-start.7 = (bf16[256,256]{1,0:T(8,128)(2,1)}, bf16[256,256]{1,0:T(8,128)(2,1)S(1)}, u32[]{:S(2)}) copy-start(bf16[256,256]{1,0:T(8,128)(2,1)S(1)} %get-tuple-element.66) | copy-start | bytes 393220
  85.5 2.0 %copy-start.9 = (bf16[256,256]{1,0:T(8,128)(2,1)}, bf16[256,256]{1,0:T(8,128)(2,1)S(1)}, u32[]{:S(2)}) copy-start(bf16[256,256]{1,0:T(8,128)(2,1)S(1)} %fusion.100) | copy-start | bytes 393220
  91.6 0.9 copy-start.21
  92.0 0.7 copy-start.22
  92.0 0.7 copy-start.23
  99.6 3.2 %copy-start.18 = (s32[512]{0:T(512)S(1)}, s32[512]{0:T(512)}, u32[]{:S(2)}) copy-start(s32[512]{0:T(512)} %get-tuple-element.6) | copy-start | bytes 6148
  99.6 3.2 %copy-start.19 = (f32[512]{0:T(512)S(1)}, f32[512]{0:T(512)}, u32[]{:S(2)}) copy-start(f32[512]{0:T(512)} %gather_fusion.1) | copy-start | bytes 6148
  99.7 3.2 %copy-start.20 = (f32[2,512]{1,0:T(2,128)S(1)}, f32[2,512]{1,0:T(2,128)}, u32[]{:S(2)}) copy-start(f32[2,512]{1,0:T(2,128)} %param.15) | copy-start | bytes 12292
  102.9 70.3 %copy-start.11 = (f32[2,512]{1,0:T(2,128)}, f32[2,512]{1,0:T(2,128)S(1)}, u32[]{:S(2)}) copy-start(f32[2,512]{1,0:T(2,128)S(1)} %maximum_subtract_fusion) | copy-start | bytes 12292
  173.2 2.5 %copy-start.8 = (bf16[256,256]{1,0:T(8,128)(2,1)S(1)}, bf16[256,256]{1,0:T(8,128)(2,1)}, u32[]{:S(2)}) copy-start(bf16[256,256]{1,0:T(8,128)(2,1)} %copy-done.7) | copy-start | bytes 393220
  173.2 2.5 %copy-start.10 = (bf16[256,256]{1,0:T(8,128)(2,1)S(1)}, bf16[256,256]{1,0:T(8,128)(2,1)}, u32[]{:S(2)}) copy-start(bf16[256,256]{1,0:T(8,128)(2,1)} %copy-done.9) | copy-start | bytes 393220
  179.6 1.0 copy-start.2
  182.0 1.5 copy-start.13
  182.0 1.5 copy-start.15
  182.0 1.5 copy-start.17
  182.0 5.8 %copy-start.6 = (bf16[256,512]{1,0:T(8,128)(2,1)S(1)}, bf16[256,512]{1,0:T(8,128)(2,1)}, u32[]{:S(2)}) copy-start(bf16[256,512]{1,0:T(8,128)(2,1)} %copy-done.5) | copy-start | bytes 786436
  187.9 3.0 %copy-start.4 = (bf16[256,512]{1,0:T(8,128)(2,1)S(1)}, bf16[256,512]{1,0:T(8,128)(2,1)}, u32[]{:S(2)}) copy-start(bf16[256,512]{1,0:T(8,128)(2,1)} %copy-done.3) | copy-start | bytes 786436
where the time goes:
time: 195 us; the launch traced here: 194 us
  blocking collectives  127 us (65%)
  other arithmetic  28.6 us (15%)
  matrix products  20.3 us (10%)
  local copies, waits for them, and re-layouts  17.1 us (9%)
    psum x1, blocking collectives, shards(): summed = lax.psum(stacked, ('frow', 'fcol'))  64.4 us
    psum x1, blocking collectives, shards(): ghat_real, ghat_imag = lax.psum((local_real, local_imag), ('frow', 'fcol'))  62.5 us
    dot_general x2, matrix products, shards(): jnp.dot(u_both.astype(bf16), jnp.concatenate([col_cos, -col_sin], 0), pre...  6.29 us
    convert_element_type x1, other arithmetic, sky_tables(): jnp.sin(angles).astype(jnp.bfloat16)  4.64 us
    convert_element_type x1, other arithmetic, sky_tables(): jnp.cos(angles).astype(jnp.bfloat16)  4.64 us
    neg x1, other arithmetic, shards(): -col_sin  4.36 us
    gather x1, local copies, waits for them, and re-layouts, shards(): jnp.take(hat_imag.reshape(-1), cell_ids)  4.27 us

commit v1 on v0

--- a/solution.py
+++ b/solution.py
@@ -98,7 +98,7 @@
     )
     local_real = jax.ops.segment_sum(residual[0], cell_ids, num_segments=cells_all)
     local_imag = jax.ops.segment_sum(residual[1], cell_ids, num_segments=cells_all)
-    ghat_real, ghat_imag = lax.psum((local_real, local_imag), ("frow", "fcol"))
+    ghat_real, ghat_imag = lax.psum(lax.psum((local_real, local_imag), "fcol"), "frow")
     ghat_both = jnp.concatenate(
         [
             ghat_real.reshape(subgrids * SG, SG).astype(bf16),

time: 195 us -> 287 us (1.47)
  waiting for transfers between devices: 0 us -> 96.8 us
  blocking collectives: 127 us -> 106 us
  between operations: 1.22 us -> 14.6 us
    psum x0 -> x1, waiting for transfers between devices: none -> 96.8 us  [shards(): lax.psum((local_real, local_imag), 'fcol')]
    psum x1, blocking collectives: 62.5 us -> 41.3 us  [shards(): lax.psum(lax.psum((local_real, local_imag), 'fcol'), 'frow')]
  transfers between devices with their start and end apart: 0 -> 1, of which waited for: 0 -> 1; matrix products, arithmetic and copies ran while one was open for 0% -> 2% of each run, Pallas kernels for 0% -> 0%
where the time goes in v1:
time: 287 us
  blocking collectives  106 us (37%)
  waiting for transfers between devices  96.8 us (34%)
  other arithmetic  31.3 us (11%)
  matrix products  21.3 us (7%)
  local copies, waits for them, and re-layouts  16.9 us (6%)
  between operations  14.6 us (5%)
    psum x1, waiting for transfers between devices, shards(): lax.psum((local_real, local_imag), 'fcol')  96.8 us
    psum x1, blocking collectives, shards(): summed = lax.psum(stacked, ('frow', 'fcol'))  64.4 us
    psum x1, blocking collectives, shards(): lax.psum(lax.psum((local_real, local_imag), 'fcol'), 'frow')  41.3 us
    dot_general x2, matrix products, shards(): jnp.dot(u_both.astype(bf16), jnp.concatenate([col_cos, -col_sin], 0), pre...  6.26 us
  transfers between devices with their start and end apart: 1, of which 1 were waited for; matrix products, arithmetic and copies ran while one was open for 2% of the time, Pallas kernels for 0%

profile of v1, /device:TPU:0, one launch (start us, length us, event | category | flops | bytes accessed | tf_op | source)
XLA Modules:
  0.0 286.5 jit_solution(15744373363774511993)
XLA Ops:
  7.2 1.3 fusion.145
  8.6 0.7 and_select_fusion.4
  9.2 0.7 and_select_fusion.2
  9.9 1.3 fusion.144
  11.2 0.7 and_select_fusion.6
  11.9 0.7 and_select_fusion
  12.6 4.6 %sine_convert_fusion.2 = (bf16[256,512]{1,0:T(8,128)(2,1)S(1)}, bf16[256,512]{1,0:T(8,128)(2,1)S(1)}, bf16[256,512]{1,0:T(8,128)(2,1)S(1)}, bf16[256,512]{1,0:T(8,128)(2,1)S(1)}) fusion(s32[512]{0:T(512)S(1)} %get-tuple-element.56, s32[256]{0:T(256)S(1)} %get-tuple-element.57, s32[512]{0:T(512)S(1)} %get-tuple-element.55, s32[256]{0:T(256)S(1)} %get-tuple-element.58, ...), kind=kLoop, calls=%fused_computation.116 | loop fusion | flops 4718592 | bytes 1056768 | tf_op jit(solution)/shard_map/convert_element_type | solution.py:22
  18.4 4.6 %cosine_convert_fusion.3 = (bf16[256,512]{1,0:T(8,128)(2,1)S(1)}, bf16[256,512]{1,0:T(8,128)(2,1)S(1)}, bf16[256,512]{1,0:T(8,128)(2,1)S(1)}, bf16[256,512]{1,0:T(8,128)(2,1)S(1)}) fusion(s32[512]{0:T(512)S(1)} %get-tuple-element.62, s32[256]{0:T(256)S(1)} %get-tuple-element.63, s32[512]{0:T(512)S(1)} %get-tuple-element.61, s32[256]{0:T(256)S(1)} %get-tuple-element.64, ...), kind=kLoop, calls=%fused_computation.123 | loop fusion | flops 4718592 | bytes 1056768 | tf_op jit(solution)/shard_map/convert_element_type | solution.py:22
  25.0 1.7 sine_convert_fusion.4
  26.7 1.6 fusion.100
  29.1 64.4 %all-reduce.7 = bf16[1024,512]{0,1:T(8,128)(2,1)} all-reduce(f32[1024,512]{0,1:T(8,128)S(1)} %pad_maximum_fusion), channel_id=1, replica_groups=mesh['frow'=4,'fcol'=8] {'frow','fcol'}, use_global_device_ids=true, to_apply=%region_0.1 | all-reduce | flops 524288 | bytes 3145728 | tf_op jit(solution)/shard_map/psum | solution.py:75
  93.6 2.0 convolution_convert_fusion.1
  95.6 1.4 convolution_bitcast_fusion.2
  97.0 1.4 convolution_bitcast_fusion.3
  98.4 1.3 fusion.9
  101.3 2.5 copy.15
  103.9 1.8 copy.23
  105.7 4.3 %gather_fusion.1 = f32[512]{0:T(512)} fusion(f32[262144]{0:T(1024)S(1)} %bitcast.67, s32[1024]{0:T(1024)S(1)} %pad_clamp_fusion), kind=kCustom, calls=%fused_computation.1.clone | custom fusion | bytes 6144 | tf_op jit(solution)/shard_map/jit(_take)/gather | solution.py:92
  109.9 3.1 %gather_fusion = f32[512]{0:T(512)S(1)} fusion(f32[262144]{0:T(1024)S(1)} %bitcast.68, s32[1024]{0:T(1024)S(1)} %pad_clamp_fusion), kind=kCustom, calls=%fused_computation.clone | custom fusion | bytes 6144 | tf_op jit(solution)/shard_map/jit(_take)/gather | solution.py:92
  113.2 4.3 %scatter_custom_fusion = f32[262144]{0:T(1024)} fusion(s32[512]{0:T(512)S(1)} %copy-done.14, f32[512]{0:T(512)S(1)} %bitcast.78, f32[]{:T(128)} %constant.156.clone.1), kind=kCustom, calls=%fused_computation.120 | custom fusion | flops 512 | bytes 1048580 | tf_op jit(solution)/shard_map/scatter-add | solution.py:99
  117.5 4.2 %scatter_custom_fusion.1 = f32[262144]{0:T(1024)} fusion(s32[512]{0:T(512)S(1)} %copy-done.14, f32[512]{0:T(512)S(1)} %bitcast.77, f32[]{:T(128)} %constant.156.clone.1), kind=kCustom, calls=%fused_computation.118 | custom fusion | flops 512 | bytes 1048580 | tf_op jit(solution)/shard_map/scatter-add | solution.py:100
  121.8 4.4 %fusion.138 = (bf16[256,512]{1,0:T(8,128)(2,1)S(1)}, bf16[256,512]{1,0:T(8,128)(2,1)S(1)}) fusion(s32[512]{0:T(512)S(1)} %get-tuple-element.56, s32[256]{0:T(256)S(1)} %copy-done.11, s32[512]{0:T(512)S(1)} %get-tuple-element.55, s32[256]{0:T(256)S(1)} %copy-done.13, s32[256]{0:T(256)S(1)} %get-tuple-element.57, s32[256]{0:T(256)S(1)} %copy-done.9), kind=kLoop, calls=%fused_computation.238 | loop fusion | flops 5242880 | bytes 532480 | tf_op jit(solution)/shard_map/neg | solution.py:129
  126.2 96.8 %all-reduce.6.cloned.1.call-done = (f32[262144]{0:T(1024)}, f32[262144]{0:T(1024)}) async-done(((f32[262144]{0:T(1024)}, f32[262144]{0:T(1024)}), (f32[262144]{0:T(1024)}, f32[262144]{0:T(1024)})) %all-reduce.6.cloned.1.call-update) | async-done | bytes 2097168 | tf_op jit(solution)/shard_map/psum | solution.py:101
  222.9 41.3 %all-reduce.8 = (bf16[262144]{0:T(1024)(128)(2,1)S(1)}, bf16[262144]{0:T(1024)(128)(2,1)S(1)}) all-reduce(f32[262144]{0:T(1024)} %get-tuple-element.3, f32[262144]{0:T(1024)} %get-tuple-element.4), channel_id=1, replica_groups=mesh['frow'=4,'fcol'=8] {'frow'}, use_global_device_ids=true, to_apply=%region_6.8 | all-reduce | flops 524288 | bytes 3145728 | tf_op jit(solution)/shard_map/psum | solution.py:101
  264.6 1.7 convolution_convert_fusion
  266.3 1.4 convolution_bitcast_fusion
  267.7 1.4 convolution_bitcast_fusion.1
  269.7 0.8 copy-done.2
  270.5 1.5 fusion.59
  272.0 1.5 fusion.36
  273.4 3.0 %fusion.3 = f32[512,512]{1,0:T(8,128)} fusion(f32[512,512]{1,0:T(8,128)} %fusion.36, bf16[256,512]{1,0:T(8,128)(2,1)S(1)} %copy-done.6, bf16[256,256]{0,1:T(8,128)(2,1)S(1)} %get-tuple-element.31, bf16[256,256]{0,1:T(8,128)(2,1)S(1)} %get-tuple-element.27, bf16[256,256]{0,1:T(8,128)(2,1)S(1)} %get-tuple-element.23, ...), kind=kOutput, calls=%fused_computation.19 | convolution fusion | flops 541589504 | bytes 3538944 | tf_op jit(solution)/shard_map/dot_general | solution.py:128
  276.4 3.3 %fusion = f32[512,512]{1,0:T(8,128)} fusion(f32[512,512]{1,0:T(8,128)} %fusion.3, f32[512,512]{1,0:T(8,128)} %fusion.59, bf16[256,512]{1,0:T(8,128)(2,1)S(1)} %copy-done.4, bf16[256,256]{0,1:T(8,128)(2,1)S(1)} %get-tuple-element.29, bf16[256,256]{0,1:T(8,128)(2,1)S(1)} %get-tuple-element.25, bf16[256,256]{0,1:T(8,128)(2,1)S(1)} %get-tuple-element.21, ...), kind=kOutput, calls=%fused_computation.12 | convolution fusion | flops 542113792 | bytes 4587520 | tf_op jit(solution)/shard_map/dot_general | solution.py:128
  (71 shorter events, 6.4 us)
Async XLA Ops:
  7.2 10.1 %copy-start = (bf16[512,512]{1,0:T(8,128)(2,1)S(1)}, bf16[512,512]{1,0:T(8,128)(2,1)}, u32[]{:S(2)}) copy-start(bf16[512,512]{1,0:T(8,128)(2,1)} %param.9) | copy-start | bytes 1572868
  7.2 215.7 %all-reduce.6.cloned.1.call-start = ((), (), s32[]{:S(2)}) async-start(), calls=%async_computation | async-start | bytes 4194304 | tf_op jit(solution)/shard_map/psum | solution.py:101
  9.2 9.2 %copy-start.8 = (s32[256]{0:T(256)}, s32[256]{0:T(256)S(1)}, u32[]{:S(2)}) copy-start(s32[256]{0:T(256)S(1)} %get-tuple-element.58) | copy-start | bytes 3076
  9.9 8.5 %copy-start.10 = (s32[256]{0:T(256)}, s32[256]{0:T(256)S(1)}, u32[]{:S(2)}) copy-start(s32[256]{0:T(256)S(1)} %get-tuple-element.59) | copy-start | bytes 3076
  9.9 8.5 %copy-start.12 = (s32[256]{0:T(256)}, s32[256]{0:T(256)S(1)}, u32[]{:S(2)}) copy-start(s32[256]{0:T(256)S(1)} %get-tuple-element.60) | copy-start | bytes 3076
  17.2 0.7 copy-start.5
  17.2 5.8 %copy-start.3 = (bf16[256,512]{1,0:T(8,128)(2,1)}, bf16[256,512]{1,0:T(8,128)(2,1)S(1)}, u32[]{:S(2)}) copy-start(bf16[256,512]{1,0:T(8,128)(2,1)S(1)} %get-tuple-element.47) | copy-start | bytes 786436
  23.1 1.0 copy-start.1
  99.7 0.9 copy-start.17
  100.1 0.7 copy-start.18
  100.1 0.7 copy-start.19
  109.9 3.2 %copy-start.14 = (s32[512]{0:T(512)S(1)}, s32[512]{0:T(512)}, u32[]{:S(2)}) copy-start(s32[512]{0:T(512)} %get-tuple-element.8) | copy-start | bytes 6148
  109.9 3.2 %copy-start.15 = (f32[512]{0:T(512)S(1)}, f32[512]{0:T(512)}, u32[]{:S(2)}) copy-start(f32[512]{0:T(512)} %gather_fusion.1) | copy-start | bytes 6148
  109.9 3.2 %copy-start.16 = (f32[2,512]{1,0:T(2,128)S(1)}, f32[2,512]{1,0:T(2,128)}, u32[]{:S(2)}) copy-start(f32[2,512]{1,0:T(2,128)} %param.15) | copy-start | bytes 12292
  113.1 8.6 %copy-start.7 = (f32[2,512]{1,0:T(2,128)}, f32[2,512]{1,0:T(2,128)S(1)}, u32[]{:S(2)}) copy-start(f32[2,512]{1,0:T(2,128)S(1)} %maximum_subtract_fusion) | copy-start | bytes 12292
  113.2 8.6 %copy-start.9 = (s32[256]{0:T(256)S(1)}, s32[256]{0:T(256)}, u32[]{:S(2)}) copy-start(s32[256]{0:T(256)} %copy-done.8) | copy-start | bytes 3076
  113.2 8.6 %copy-start.11 = (s32[256]{0:T(256)S(1)}, s32[256]{0:T(256)}, u32[]{:S(2)}) copy-start(s32[256]{0:T(256)} %copy-done.10) | copy-start | bytes 3076
  113.2 8.6 %copy-start.13 = (s32[256]{0:T(256)S(1)}, s32[256]{0:T(256)}, u32[]{:S(2)}) copy-start(s32[256]{0:T(256)} %copy-done.12) | copy-start | bytes 3076
  269.6 1.0 copy-start.2
  272.0 1.5 copy-start.6
  273.4 3.0 %copy-start.4 = (bf16[256,512]{1,0:T(8,128)(2,1)S(1)}, bf16[256,512]{1,0:T(8,128)(2,1)}, u32[]{:S(2)}) copy-start(bf16[256,512]{1,0:T(8,128)(2,1)} %copy-done.3) | copy-start | bytes 786436
Sparse Core Ops, SparseCore 0:
  121.9 101.0 all-reduce.5
